TPU v7x, 32 devices: a whole 2x2x4 slice. The times are simulated.
32 devices in a mesh: group: 2 (over y), seq: 4 (over z), shard: 2 (over x), guide: 2 (over core).
Axes of the slice: x: 2, y: 2, z: 4, core: 2. Of those that a mesh axis runs over, the one named last changes fastest.
Arguments:
- queries: bfloat16 [2, 2, 512, 2560], P('guide', 'group', 'seq', 'shard'), parts along dimension 1, may hold values from -120 to 120
- key_vecs: bfloat16 [2, 2, 512, 2560], P('guide', 'group', 'seq', 'shard'), parts along dimension 1, may hold values from -4 to 4
- value_vecs: bfloat16 [2, 2, 512, 2560], P('guide', 'group', 'seq', 'shard'), parts along dimension 1, may hold values from -24 to 24
- residual: bfloat16 [2, 2, 512, 5120], P('guide', 'group', 'seq', 'shard'), parts along dimension 1, may hold values from -64 to 64
- w_out: bfloat16 [2560, 5120], P('shard', 'guide'), may hold values from -0.125 to 0.125
- attn_gate: float32 [2, 5120], P('group', 'shard'), parts along dimension 0, may hold values from 2 to 4
- norm_shift: float32 [2, 5120], P('group', 'shard'), parts along dimension 0, may hold values from -3 to 3
- norm_scale: float32 [2, 5120], P('group', 'shard'), parts along dimension 0, may hold values from -2.5 to 2.5
- w_head: bfloat16 [5120, 64], P('shard'), may hold values from -0.078125 to 0.078125
- noise: float32 [2, 4, 128, 64], P('group', 'seq', None, 'guide'), parts along dimension 0, may hold values from -6 to 6
- timesteps: int32 [2], P('group'), parts along dimension 0, may hold values from 100 to 980
- frame_owner: int32 [2, 4], P('group'), parts along dimension 0, may hold values from 0 to 3, each once within a row
Outputs:
- sds_grad: float32 [2, 4, 128, 64], P('group', 'seq', None, 'guide'), parts along dimension 0
There are 2 independent parts, one for each index of `group`. A program takes and returns all parts, laid end to end along the dimension named above; an argument that names none is the same for every part. Nothing has to cross between parts.
Inputs may be any that keep to these rules, and one draw needn't show every extreme that they name: `frame_owner`: each row names every owner index once.
All inputs are finite; a program needn't handle non-finite values.
Results may differ from a plain program's by a relative error of at most 0.003.
Values may be sent and summed in bfloat16 or wider, within the bound.
No kernel may reach another device: no remote copies, remote signals or barrier semaphores. Data moves between devices by JAX's collectives and lax.ppermute only.
A program may use at most 128 MiB of HBM per device.

v0:
```python
import jax
import jax.numpy as jnp
from jax import lax
from jax.sharding import PartitionSpec as P

D = 5120
HEAD_DIM = 128
beta_low = 0.0001
beta_high = 0.02
guidance_scale = 3.0
norm_epsilon = 1e-06


def plan_weight(timesteps):
    steps_float = timesteps.astype(jnp.float32)
    exponent = (steps_float + 1.0) * beta_low + (beta_high - beta_low) * steps_float * (
        steps_float + 1.0
    ) / (2.0 * 999.0)
    return 1.0 - jnp.exp(-exponent)


def softmax_absorb(query_block, carry_state, pieces):
    running_top, running_total, running_acc = carry_state
    keys_block, values_block = pieces
    heads_local = query_block.shape[2]
    keys_split = keys_block.reshape(keys_block.shape[0], keys_block.shape[1], heads_local, HEAD_DIM)
    values_split = values_block.reshape(
        values_block.shape[0], values_block.shape[1], heads_local, HEAD_DIM
    )
    scores = jnp.einsum(
        "tqhd,tkhd->tqhk", query_block, keys_split, preferred_element_type=jnp.float32
    ) * HEAD_DIM ** (-0.5)
    new_top = jnp.max(scores, axis=-1)
    factor = jnp.exp(running_top - new_top)
    expo = jnp.exp(scores - new_top[..., None])
    new_total = running_total * factor + jnp.sum(expo, axis=-1)
    update = jnp.einsum(
        "tqhk,tkhd->tqhd",
        expo.astype(jnp.bfloat16),
        values_split,
        preferred_element_type=jnp.float32,
    )
    return (new_top, new_total, running_acc * factor[..., None] + update)


def start_state(step_count, token_count, heads_local):
    return (
        jnp.full((step_count, token_count, heads_local), -jnp.inf, jnp.float32),
        jnp.zeros((step_count, token_count, heads_local), jnp.float32),
        jnp.zeros((step_count, token_count, heads_local, HEAD_DIM), jnp.float32),
    )


def on_device(
    queries,
    key_vecs,
    value_vecs,
    residual,
    w_out,
    attn_gate,
    norm_shift,
    norm_scale,
    w_head,
    noise,
    timesteps,
    frame_owner,
):
    query_local = queries[0]
    step_count, token_count, width_local = query_local.shape
    heads_local = width_local // HEAD_DIM
    query_split = query_local.reshape(step_count, token_count, heads_local, HEAD_DIM)
    final_state = softmax_absorb(
        query_split,
        start_state(step_count, token_count, heads_local),
        (
            lax.all_gather(key_vecs[0], "seq", axis=1, tiled=True),
            lax.all_gather(value_vecs[0], "seq", axis=1, tiled=True),
        ),
    )
    total_sum = final_state[1]
    acc_sum = final_state[2]
    row_count = step_count * token_count
    attended = (acc_sum / total_sum[..., None]).astype(jnp.bfloat16).reshape(row_count, width_local)
    both_rows = jnp.dot(
        lax.all_gather(attended, "guide", axis=0, tiled=True),
        w_out,
        preferred_element_type=jnp.float32,
    )
    half_width = w_out.shape[1]
    swapped = lax.all_to_all(
        both_rows.reshape(2, row_count, half_width),
        "guide",
        split_axis=0,
        concat_axis=2,
        tiled=True,
    )
    projected = swapped.reshape(row_count, 2 * half_width)
    attn_out = lax.psum_scatter(projected, "shard", scatter_dimension=1, tiled=True)
    width_shard = attn_out.shape[1]
    hidden = residual[0].astype(jnp.float32) + attn_gate[:, None, :] * attn_out.reshape(
        step_count, token_count, width_shard
    )
    sum_first = jnp.sum(hidden, axis=-1)
    sum_second = jnp.sum(hidden * hidden, axis=-1)
    sum_first, sum_second = lax.psum((sum_first, sum_second), "shard")
    mean_row = sum_first / D
    var_row = sum_second / D - mean_row * mean_row
    inv_std = lax.rsqrt(var_row + norm_epsilon)
    modulated = (hidden - mean_row[..., None]) * inv_std[..., None] * (
        1.0 + norm_scale[:, None, :]
    ) + norm_shift[:, None, :]
    head_float = w_head.astype(jnp.float32)
    partial_head = jnp.einsum("tqd,dc->tqc", modulated, head_float, precision=lax.Precision.HIGHEST)
    predicted = lax.psum(partial_head, "shard")
    seq_count = lax.axis_size("seq")
    frame_group = token_count // seq_count
    channels = predicted.shape[-1]
    frames_view = predicted.reshape(step_count, seq_count, frame_group, channels)
    owner_table = (
        frame_owner[:, :, None] == jnp.arange(seq_count, dtype=jnp.int32)[None, None, :]
    ).astype(jnp.float32)
    by_owner = jnp.einsum(
        "tfo,tfgc->togc", owner_table, frames_view, precision=lax.Precision.HIGHEST
    )
    weight = plan_weight(timesteps)
    arrived = lax.all_to_all(
        lax.all_to_all(by_owner[None], "seq", split_axis=2, concat_axis=3, tiled=True),
        "guide",
        split_axis=4,
        concat_axis=0,
        tiled=True,
    )
    guided = arrived[1] + guidance_scale * (arrived[0] - arrived[1])
    return weight[:, None, None, None] * (guided - noise)


def solution(mesh):
    return jax.shard_map(
        on_device,
        mesh=mesh,
        in_specs=(
            P("guide", "group", "seq", "shard"),
            P("guide", "group", "seq", "shard"),
            P("guide", "group", "seq", "shard"),
            P("guide", "group", "seq", "shard"),
            P("shard", "guide"),
            P("group", "shard"),
            P("group", "shard"),
            P("group", "shard"),
            P("shard", None),
            P("group", "seq", None, "guide"),
            P("group"),
            P("group", None),
        ),
        out_specs=P("group", "seq", None, "guide"),
        check_vma=False,
    )
```

profile of v0, /device:TPU:0, one launch (start us, length us, event | category | flops | bytes accessed | tf_op | source)
XLA Modules:
  0.0 175.5 jit_solution(11851235863250960437)
XLA Ops:
  6.5 0.0 copy-start
  6.5 0.0 copy-start.3
  6.5 0.0 all-gather.5.cloned.1.call-start
  6.5 1.9 %copy.44 = bf16[1,1,128,1280]{2,3,1,0:T(8,128)(2,1)} copy(bf16[1,1,128,1280]{3,2,1,0:T(8,128)(2,1)} %param.13) | data formatting | bytes 655360 | tf_op args[1]
  8.5 0.0 all-gather.5.cloned.1.call-update
  8.5 0.0 all-gather.7.cloned.1.call-start
  8.5 0.7 all-gather.7.cloned.1.call-update
  9.2 0.0 reduce-scatter.2.cloned.1.call-start
  9.3 0.0 copy-done.3
  9.3 0.2 copy.45
  9.5 35.6 %all-gather.5.cloned.1.call-done = bf16[1,1,512,1280]{2,3,1,0:T(8,128)(2,1)} async-done(((bf16[1,1,128,1280]{2,3,1,0:T(8,128)(2,1)}), bf16[1,1,512,1280]{2,3,1,0:T(8,128)(2,1)}) %all-gather.5.cloned.1.call-update) | async-done | bytes 1310736 | tf_op jit(solution)/shard_map/all_gather | solution.py:76
  45.1 1.9 %bitcast_reduce_fusion = (f32[128,10]{0,1:T(8,128)S(1)}, f32[10,512,128]{2,1,0:T(8,128)S(1)}) fusion(bf16[512,10,128]{0,2,1:T(8,128)(2,1)} %bitcast.120, bf16[128,10,128]{0,2,1:T(8,128)(2,1)S(1)} %bitcast.119), kind=kOutput, calls=%fused_computation.1 | convolution fusion | flops 169081600 | bytes 4264960 | tf_op jit(solution)/shard_map/tqhd,tkhd->tqhk/dot_general | solution.py:30
  47.0 0.4 fusion.1
  47.5 30.0 %all-gather.7.cloned.1.call-done = bf16[1,1,512,1280]{3,2,1,0:T(8,128)(2,1)} async-done(((bf16[1,1,128,1280]{3,2,1,0:T(8,128)(2,1)}), bf16[1,1,512,1280]{3,2,1,0:T(8,128)(2,1)}) %all-gather.7.cloned.1.call-update) | async-done | bytes 1310736 | tf_op jit(solution)/shard_map/all_gather | solution.py:77
  77.5 2.4 %copy.48 = bf16[1,1,512,1280]{2,3,1,0:T(8,128)(2,1)} copy(bf16[1,1,512,1280]{3,2,1,0:T(8,128)(2,1)} %all-gather.7.cloned.1.call-done) | data formatting | bytes 2621440 | tf_op jit(solution)/shard_map/all_gather | solution.py:77
  79.9 2.1 %fusion.22 = bf16[1,128,10,128]{1,3,2,0:T(8,128)(2,1)S(1)} fusion(bf16[512,10,128]{0,2,1:T(8,128)(2,1)} %bitcast.121, f32[10,512,128]{2,1,0:T(8,128)S(1)} %get-tuple-element.14, f32[128,10]{0,1:T(8,128)S(1)} %get-tuple-element.13, f32[128,10]{0,1:T(8,128)S(1)} %get-tuple-element.10, f32[128,10]{0,1:T(8,128)S(1)} %get-tuple-element.9), kind=kOutput, calls=%fused_computation.19 | convolution fusion | flops 170229760 | bytes 4275200 | tf_op jit(solution)/shard_map/tqhk,tkhd->tqhd/dot_general | solution.py:37
  82.0 2.3 %all_gather.11 = bf16[256,1280]{0,1:T(8,128)(2,1)S(1)} all-gather(bf16[128,1280]{0,1:T(8,128)(2,1)S(1)} %bitcast.122), channel_id=1, replica_groups=mesh['group'=2,'seq'=4,'shard'=2,'guide'=2] {'guide'}, dimensions={0}, use_global_device_ids=true | all-gather | bytes 983040 | tf_op jit(solution)/shard_map/all_gather | solution.py:85
  84.3 4.7 %fusion.40 = f32[256,2560]{1,0:T(8,128)S(1)} fusion(bf16[256,1280]{0,1:T(8,128)(2,1)S(1)} %all_gather.11, bf16[1280,2560]{1,0:T(8,128)(2,1)} %param.16), kind=kOutput, calls=%fused_computation.43 | convolution fusion | flops 1677721600 | bytes 9830400 | tf_op jit(solution)/shard_map/dot_general | solution.py:84
  89.1 5.8 %all_to_all.42 = f32[2,128,2560]{2,1,0:T(8,128)S(1)} all-to-all(f32[2,128,2560]{2,1,0:T(8,128)S(1)} %bitcast.115), channel_id=1, replica_groups=mesh['group'=2,'seq'=4,'shard'=2,'guide'=2] {'guide'}, dimensions={0} | all-to-all | bytes 5242880 | tf_op jit(solution)/shard_map/all_to_all | solution.py:90
  94.9 2.0 %copy.50 = f32[1,128,2,2560]{3,2,1,0:T(2,128)S(1)} copy(f32[1,128,2,2560]{3,1,2,0:T(8,128)S(1)} %bitcast.117) | data formatting | bytes 5242880 | tf_op jit(solution)/shard_map/all_to_all | solution.py:90
  96.9 2.0 %copy.63 = f32[16,8,2,2560]{3,1,2,0:T(8,128)} copy(f32[16,8,2,2560]{3,2,1,0:T(2,128)S(1)} %bitcast.118) | data formatting | bytes 5242880
  98.9 0.0 copy-start.5
  98.9 0.0 reduce-scatter.2.cloned.1.call-update
  98.9 0.7 copy-done.5
  99.6 0.0 copy-done.6
  99.7 0.0 copy-done.7
  99.7 36.1 %reduce-scatter.2.cloned.1.call-done = f32[128,2560]{1,0:T(8,128)} async-done(((f32[128,5120]{1,0:T(8,128)}), f32[128,2560]{1,0:T(8,128)}) %reduce-scatter.2.cloned.1.call-update) | async-done | bytes 1310736 | tf_op jit(solution)/shard_map/reduce_scatter | solution.py:98
  135.9 0.0 copy-done.2
  135.9 1.8 %fusion.29 = (f32[128]{0:T(128)S(1)}, f32[128]{0:T(128)S(1)}) fusion(f32[128,2560]{1,0:T(8,128)} %reduce-scatter.2.cloned.1.call-done, f32[2560]{0:T(1024)S(1)} %reduce.6, bf16[1,1,128,2560]{3,2,1,0:T(8,128)(2,1)S(1)} %copy-done.2), kind=kLoop, calls=%fused_computation.25 | loop fusion | flops 1965824 | bytes 1977344 | tf_op jit(solution)/shard_map/reduce_sum | solution.py:103
  137.6 4.9 %all-reduce = (f32[1,128]{1,0:T(1,128)S(1)}, f32[1,128]{1,0:T(1,128)S(1)}) all-reduce(f32[1,128]{1,0:T(1,128)S(1)} %bitcast.130, f32[1,128]{1,0:T(1,128)S(1)} %bitcast.129), channel_id=1, replica_groups=mesh['group'=2,'seq'=4,'shard'=2,'guide'=2] {'shard'}, use_global_device_ids=true, to_apply=%region_6.0 | all-reduce | flops 256 | bytes 2048 | tf_op jit(solution)/shard_map/psum | solution.py:105
  142.6 0.0 copy-done
  142.6 0.0 copy-done.1
  142.6 0.0 copy-start.8
  142.6 0.0 copy-start.4
  142.6 1.0 fusion.6
  143.7 7.8 %psum.23 = f32[4,32,64]{2,0,1:T(4,128)S(1)} all-reduce(f32[4,32,64]{2,0,1:T(4,128)S(1)} %copy.52), channel_id=1, replica_groups=mesh['group'=2,'seq'=4,'shard'=2,'guide'=2] {'shard'}, use_global_device_ids=true, to_apply=%region_7.0 | all-reduce | flops 8192 | bytes 65536 | tf_op jit(solution)/shard_map/psum | solution.py:114
  151.5 0.0 copy-done.8
  151.5 0.3 convolution_bitcast_fusion
  151.8 0.7 reshape.232
  152.5 5.0 %all-to-all-start.1 = ((f32[4,1,2048]{2,1,0:T(1,128)}), f32[4,1,2048]{2,1,0:T(1,128)S(1)}, u32[]{:S(2)}, u32[]{:S(2)}) async-start(f32[4,1,2048]{2,1,0:T(1,128)} %reshape.232), calls=%async_computation.2 | async-start | bytes 65536 | tf_op jit(solution)/shard_map/all_to_all | solution.py:127
  158.2 5.0 %all-to-all-done.1 = f32[4,1,2048]{2,1,0:T(1,128)S(1)} async-done(((f32[4,1,2048]{2,1,0:T(1,128)}), f32[4,1,2048]{2,1,0:T(1,128)S(1)}, u32[]{:S(2)}, u32[]{:S(2)}) %all-to-all-start.1) | async-done | bytes 32800 | tf_op jit(solution)/shard_map/all_to_all | solution.py:127
  163.2 0.5 broadcast.99
  163.7 0.7 reduce.10
  164.4 0.1 reshape.233
  164.5 0.1 copy.55
  164.6 3.8 %all_to_all.43 = f32[1,1,1,128,64]{3,2,1,0,4:T(1,128)S(1)} all-to-all(f32[1,1,1,128,64]{3,2,1,0,4:T(1,128)S(1)} %copy.55), channel_id=1, replica_groups=mesh['group'=2,'seq'=4,'shard'=2,'guide'=2] {'guide'}, dimensions={4} | all-to-all | bytes 65536 | tf_op jit(solution)/shard_map/all_to_all | solution.py:126
  168.4 0.0 copy-done.4
  168.4 0.6 fusion.34
  (11 shorter events, 0.2 us)
Async XLA Ops:
  6.5 136.0 %copy-start = (bf16[2560,64]{0,1:T(8,128)(2,1)S(1)}, bf16[2560,64]{0,1:T(8,128)(2,1)}, u32[]{:S(2)}) copy-start(bf16[2560,64]{0,1:T(8,128)(2,1)} %param.20) | copy-start | bytes 983044
  6.5 2.8 %copy-start.3 = (bf16[1,1,128,1280]{3,2,1,0:T(8,128)(2,1)S(1)}, bf16[1,1,128,1280]{3,2,1,0:T(8,128)(2,1)}, u32[]{:S(2)}) copy-start(bf16[1,1,128,1280]{3,2,1,0:T(8,128)(2,1)} %param.12) | copy-start | bytes 983044
  6.5 38.6 %all-gather.5.cloned.1.call-start = ((), (), s32[]{:S(2)}) async-start(), calls=%async_computation.5 | async-start | bytes 1638400 | tf_op jit(solution)/shard_map/all_gather | solution.py:76
  8.5 69.0 %all-gather.7.cloned.1.call-start = ((), (), s32[]{:S(2)}) async-start(), calls=%async_computation.6 | async-start | bytes 1638400 | tf_op jit(solution)/shard_map/all_gather | solution.py:77
  9.2 126.6 %reduce-scatter.2.cloned.1.call-start = ((), (), s32[]{:S(2)}) async-start(), calls=%async_computation.4 | async-start | bytes 3932160 | tf_op jit(solution)/shard_map/reduce_scatter | solution.py:98
  98.9 0.7 copy-start.5
  98.9 0.7 copy-start.6
  98.9 0.8 copy-start.7
  98.9 37.0 %copy-start.2 = (bf16[1,1,128,2560]{3,2,1,0:T(8,128)(2,1)S(1)}, bf16[1,1,128,2560]{3,2,1,0:T(8,128)(2,1)}, u32[]{:S(2)}) copy-start(bf16[1,1,128,2560]{3,2,1,0:T(8,128)(2,1)} %param.15) | copy-start | bytes 1966084
  135.9 6.7 %copy-start.1 = (f32[128,2560]{1,0:T(8,128)S(1)}, f32[128,2560]{1,0:T(8,128)}, u32[]{:S(2)}) copy-start(f32[128,2560]{1,0:T(8,128)} %reduce-scatter.2.cloned.1.call-done) | copy-start | bytes 3932164
  142.6 8.9 %copy-start.8 = (s32[1,4]{1,0:T(1,128)S(1)}, s32[1,4]{1,0:T(1,128)}, u32[]{:S(2)}) copy-start(s32[1,4]{1,0:T(1,128)} %param.23) | copy-start | bytes 52
  142.6 25.8 %copy-start.4 = (f32[1,1,128,32]{2,3,1,0:T(8,128)S(1)}, f32[1,1,128,32]{2,3,1,0:T(8,128)}, u32[]{:S(2)}) copy-start(f32[1,1,128,32]{2,3,1,0:T(8,128)} %param.21) | copy-start | bytes 49156
  152.5 10.7 %all-to-all-start.1 = ((f32[4,1,2048]{2,1,0:T(1,128)}), f32[4,1,2048]{2,1,0:T(1,128)S(1)}, u32[]{:S(2)}, u32[]{:S(2)}) async-start(f32[4,1,2048]{2,1,0:T(1,128)} %reshape.232), calls=%async_computation.2 | async-start | bytes 65536 | tf_op jit(solution)/shard_map/all_to_all | solution.py:127
Sparse Core Ops, SparseCore 0:
  8.9 36.1 all-gather.4
  46.7 30.7 all-gather.6
  99.0 36.7 reduce-scatter.1
where the time goes:
time: 176 us
  waiting for transfers between devices  107 us (61%)
  blocking collectives  24.6 us (14%)
  between operations  14 us (8%)
  local copies, waits for them, and re-layouts  10.7 us (6%)
  matrix products  10.1 us (6%)
  starting transfers between devices  5.09 us (3%)
  other arithmetic  3.65 us (2%)
    reduce_scatter x1, waiting for transfers between devices, on_device(): lax.psum_scatter(projected, 'shard', scatter_dimension=1, tiled=True)  36.1 us
    all_gather x1, waiting for transfers between devices, on_device(): lax.all_gather(key_vecs[0], 'seq', axis=1, tiled=True)  35.6 us
    all_gather x1, waiting for transfers between devices, on_device(): lax.all_gather(value_vecs[0], 'seq', axis=1, tiled=True)  30 us
    psum x1, blocking collectives, on_device(): predicted = lax.psum(partial_head, 'shard')  7.79 us
    all_to_all x1, blocking collectives, on_device(): lax.all_to_all(both_rows.reshape(2, row_count, half_width), 'guide', spli...  5.84 us
    unnamed x23, local copies, waits for them, and re-layouts  5.6 us
    all_to_all x1, starting transfers between devices, on_device(): lax.all_to_all(by_owner[None], 'seq', split_axis=2, concat_axis=3, tiled=...  5.01 us
    all_to_all x1, waiting for transfers between devices, on_device(): lax.all_to_all(by_owner[None], 'seq', split_axis=2, concat_axis=3, tiled=...  4.96 us
  transfers between devices with their start and end apart: 4, of which 4 were waited for; matrix products, arithmetic and copies ran while one was open for 2% of the time, Pallas kernels for 0%

commit v1 on v0

--- a/solution.py
+++ b/solution.py
@@ -124,7 +124,12 @@
     )
     weight = plan_weight(timesteps)
     arrived = lax.all_to_all(
-        lax.all_to_all(by_owner[None], "seq", split_axis=2, concat_axis=3, tiled=True),
+        jnp.concatenate(
+            lax.all_to_all(
+                jnp.stack(jnp.split(by_owner[None], lax.axis_size("seq"), axis=2)), "seq", 0, 0
+            ),
+            axis=3,
+        ),
         "guide",
         split_axis=4,
         concat_axis=0,

time: 176 us -> 176 us (level)
  no operation moved by 1% of the time
where the time goes in v1:
time: 176 us
  waiting for transfers between devices  107 us (61%)
  blocking collectives  24.6 us (14%)
  between operations  14 us (8%)
  local copies, waits for them, and re-layouts  10.7 us (6%)
  matrix products  10.1 us (6%)
  starting transfers between devices  5.09 us (3%)
  other arithmetic  3.66 us (2%)
    reduce_scatter x1, waiting for transfers between devices, on_device(): lax.psum_scatter(projected, 'shard', scatter_dimension=1, tiled=True)  36.1 us
    all_gather x1, waiting for transfers between devices, on_device(): lax.all_gather(key_vecs[0], 'seq', axis=1, tiled=True)  35.6 us
    all_gather x1, waiting for transfers between devices, on_device(): lax.all_gather(value_vecs[0], 'seq', axis=1, tiled=True)  30 us
    psum x1, blocking collectives, on_device(): predicted = lax.psum(partial_head, 'shard')  7.79 us
    all_to_all x1, blocking collectives, on_device(): lax.all_to_all(both_rows.reshape(2, row_count, half_width), 'guide', spli...  5.84 us
    unnamed x23, local copies, waits for them, and re-layouts  5.6 us
    all_to_all x1, starting transfers between devices, on_device(): lax.all_to_all(jnp.stack(jnp.split(by_owner[None], lax.axis_size('seq'),...  5.01 us
    all_to_all x1, waiting for transfers between devices, on_device(): lax.all_to_all(jnp.stack(jnp.split(by_owner[None], lax.axis_size('seq'),...  4.96 us
  transfers between devices with their start and end apart: 4, of which 4 were waited for; matrix products, arithmetic and copies ran while one was open for 2% of the time, Pallas kernels for 0%

profile of v1, /device:TPU:0, one launch (start us, length us, event | category | flops | bytes accessed | tf_op | source)
XLA Modules:
  0.0 175.6 jit_solution(10513460272092350145)
XLA Ops:
  6.5 0.0 copy-start
  6.5 0.0 copy-start.3
  6.5 0.0 all-gather.5.cloned.1.call-start
  6.5 1.9 %copy.37 = bf16[1,1,128,1280]{2,3,1,0:T(8,128)(2,1)} copy(bf16[1,1,128,1280]{3,2,1,0:T(8,128)(2,1)} %param.13) | data formatting | bytes 655360 | tf_op args[1]
  8.5 0.0 all-gather.5.cloned.1.call-update
  8.5 0.0 all-gather.7.cloned.1.call-start
  8.5 0.7 all-gather.7.cloned.1.call-update
  9.2 0.0 reduce-scatter.2.cloned.1.call-start
  9.3 0.0 copy-done.3
  9.3 0.2 copy.38
  9.5 35.6 %all-gather.5.cloned.1.call-done = bf16[1,1,512,1280]{2,3,1,0:T(8,128)(2,1)} async-done(((bf16[1,1,128,1280]{2,3,1,0:T(8,128)(2,1)}), bf16[1,1,512,1280]{2,3,1,0:T(8,128)(2,1)}) %all-gather.5.cloned.1.call-update) | async-done | bytes 1310736 | tf_op jit(solution)/shard_map/all_gather | solution.py:76
  45.1 1.9 %bitcast_reduce_fusion = (f32[128,10]{0,1:T(8,128)S(1)}, f32[10,512,128]{2,1,0:T(8,128)S(1)}) fusion(bf16[512,10,128]{0,2,1:T(8,128)(2,1)} %bitcast.126, bf16[128,10,128]{0,2,1:T(8,128)(2,1)S(1)} %bitcast.125), kind=kOutput, calls=%fused_computation.1 | convolution fusion | flops 169081600 | bytes 4264960 | tf_op jit(solution)/shard_map/tqhd,tkhd->tqhk/dot_general | solution.py:30
  47.0 0.4 fusion.1
  47.5 30.0 %all-gather.7.cloned.1.call-done = bf16[1,1,512,1280]{3,2,1,0:T(8,128)(2,1)} async-done(((bf16[1,1,128,1280]{3,2,1,0:T(8,128)(2,1)}), bf16[1,1,512,1280]{3,2,1,0:T(8,128)(2,1)}) %all-gather.7.cloned.1.call-update) | async-done | bytes 1310736 | tf_op jit(solution)/shard_map/all_gather | solution.py:77
  77.5 2.4 %copy.41 = bf16[1,1,512,1280]{2,3,1,0:T(8,128)(2,1)} copy(bf16[1,1,512,1280]{3,2,1,0:T(8,128)(2,1)} %all-gather.7.cloned.1.call-done) | data formatting | bytes 2621440 | tf_op jit(solution)/shard_map/all_gather | solution.py:77
  79.9 2.1 %fusion.22 = bf16[1,128,10,128]{1,3,2,0:T(8,128)(2,1)S(1)} fusion(bf16[512,10,128]{0,2,1:T(8,128)(2,1)} %bitcast.127, f32[10,512,128]{2,1,0:T(8,128)S(1)} %get-tuple-element.18, f32[128,10]{0,1:T(8,128)S(1)} %get-tuple-element.17, f32[128,10]{0,1:T(8,128)S(1)} %get-tuple-element.14, f32[128,10]{0,1:T(8,128)S(1)} %get-tuple-element.13), kind=kOutput, calls=%fused_computation.19 | convolution fusion | flops 170229760 | bytes 4275200 | tf_op jit(solution)/shard_map/tqhk,tkhd->tqhd/dot_general | solution.py:37
  82.0 2.3 %all_gather.11 = bf16[256,1280]{0,1:T(8,128)(2,1)S(1)} all-gather(bf16[128,1280]{0,1:T(8,128)(2,1)S(1)} %bitcast.128), channel_id=1, replica_groups=mesh['group'=2,'seq'=4,'shard'=2,'guide'=2] {'guide'}, dimensions={0}, use_global_device_ids=true | all-gather | bytes 983040 | tf_op jit(solution)/shard_map/all_gather | solution.py:85
  84.3 4.7 %fusion.41 = f32[256,2560]{1,0:T(8,128)S(1)} fusion(bf16[256,1280]{0,1:T(8,128)(2,1)S(1)} %all_gather.11, bf16[1280,2560]{1,0:T(8,128)(2,1)} %param.16), kind=kOutput, calls=%fused_computation.44 | convolution fusion | flops 1677721600 | bytes 9830400 | tf_op jit(solution)/shard_map/dot_general | solution.py:84
  89.1 5.8 %all_to_all.35 = f32[2,128,2560]{2,1,0:T(8,128)S(1)} all-to-all(f32[2,128,2560]{2,1,0:T(8,128)S(1)} %bitcast.121), channel_id=1, replica_groups=mesh['group'=2,'seq'=4,'shard'=2,'guide'=2] {'guide'}, dimensions={0} | all-to-all | bytes 5242880 | tf_op jit(solution)/shard_map/all_to_all | solution.py:90
  94.9 2.0 %copy.43 = f32[1,128,2,2560]{3,2,1,0:T(2,128)S(1)} copy(f32[1,128,2,2560]{3,1,2,0:T(8,128)S(1)} %bitcast.123) | data formatting | bytes 5242880 | tf_op jit(solution)/shard_map/all_to_all | solution.py:90
  96.9 2.0 %copy.61 = f32[16,8,2,2560]{3,1,2,0:T(8,128)} copy(f32[16,8,2,2560]{3,2,1,0:T(2,128)S(1)} %bitcast.124) | data formatting | bytes 5242880
  98.9 0.0 copy-start.5
  98.9 0.0 reduce-scatter.2.cloned.1.call-update
  98.9 0.7 copy-done.5
  99.6 0.0 copy-done.6
  99.7 0.0 copy-done.7
  99.7 36.1 %reduce-scatter.2.cloned.1.call-done = f32[128,2560]{1,0:T(8,128)} async-done(((f32[128,5120]{1,0:T(8,128)}), f32[128,2560]{1,0:T(8,128)}) %reduce-scatter.2.cloned.1.call-update) | async-done | bytes 1310736 | tf_op jit(solution)/shard_map/reduce_scatter | solution.py:98
  135.9 0.0 copy-done.2
  135.9 1.8 %fusion.29 = (f32[128]{0:T(128)S(1)}, f32[128]{0:T(128)S(1)}) fusion(f32[128,2560]{1,0:T(8,128)} %reduce-scatter.2.cloned.1.call-done, f32[2560]{0:T(1024)S(1)} %reduce.6, bf16[1,1,128,2560]{3,2,1,0:T(8,128)(2,1)S(1)} %copy-done.2), kind=kLoop, calls=%fused_computation.25 | loop fusion | flops 1965824 | bytes 1977344 | tf_op jit(solution)/shard_map/reduce_sum | solution.py:103
  137.6 4.9 %all-reduce = (f32[1,128]{1,0:T(1,128)S(1)}, f32[1,128]{1,0:T(1,128)S(1)}) all-reduce(f32[1,128]{1,0:T(1,128)S(1)} %bitcast.138, f32[1,128]{1,0:T(1,128)S(1)} %bitcast.137), channel_id=1, replica_groups=mesh['group'=2,'seq'=4,'shard'=2,'guide'=2] {'shard'}, use_global_device_ids=true, to_apply=%region_6.0 | all-reduce | flops 256 | bytes 2048 | tf_op jit(solution)/shard_map/psum | solution.py:105
  142.6 0.0 copy-done
  142.6 0.0 copy-done.1
  142.6 0.0 copy-start.8
  142.6 0.0 copy-start.4
  142.6 1.0 fusion.6
  143.7 7.8 %psum.23 = f32[4,32,64]{2,0,1:T(4,128)S(1)} all-reduce(f32[4,32,64]{2,0,1:T(4,128)S(1)} %copy.45), channel_id=1, replica_groups=mesh['group'=2,'seq'=4,'shard'=2,'guide'=2] {'shard'}, use_global_device_ids=true, to_apply=%region_7.0 | all-reduce | flops 8192 | bytes 65536 | tf_op jit(solution)/shard_map/psum | solution.py:114
  151.5 0.0 copy-done.8
  151.5 0.3 convolution_bitcast_fusion
  151.9 0.7 reshape.233
  152.6 5.0 %all-to-all-start.1 = ((f32[4,1,2048]{2,1,0:T(1,128)}), f32[4,1,2048]{2,1,0:T(1,128)S(1)}, u32[]{:S(2)}, u32[]{:S(2)}) async-start(f32[4,1,2048]{2,1,0:T(1,128)} %reshape.233), calls=%async_computation.2 | async-start | bytes 65536 | tf_op jit(solution)/shard_map/all_to_all | solution.py:128
  158.3 5.0 %all-to-all-done.1 = f32[4,1,2048]{2,1,0:T(1,128)S(1)} async-done(((f32[4,1,2048]{2,1,0:T(1,128)}), f32[4,1,2048]{2,1,0:T(1,128)S(1)}, u32[]{:S(2)}, u32[]{:S(2)}) %all-to-all-start.1) | async-done | bytes 32800 | tf_op jit(solution)/shard_map/all_to_all | solution.py:128
  163.3 0.5 broadcast.99
  163.8 0.7 reduce.10
  164.5 0.1 reshape.234
  164.6 0.1 copy.50
  164.7 3.8 %all_to_all.36 = f32[1,1,1,128,64]{3,2,1,0,4:T(1,128)S(1)} all-to-all(f32[1,1,1,128,64]{3,2,1,0,4:T(1,128)S(1)} %copy.50), channel_id=1, replica_groups=mesh['group'=2,'seq'=4,'shard'=2,'guide'=2] {'guide'}, dimensions={4} | all-to-all | bytes 65536 | tf_op jit(solution)/shard_map/all_to_all | solution.py:126
  168.4 0.0 copy-done.4
  168.4 0.6 fusion.34
  (12 shorter events, 0.2 us)
Async XLA Ops:
  6.5 136.0 %copy-start = (bf16[2560,64]{0,1:T(8,128)(2,1)S(1)}, bf16[2560,64]{0,1:T(8,128)(2,1)}, u32[]{:S(2)}) copy-start(bf16[2560,64]{0,1:T(8,128)(2,1)} %param.20) | copy-start | bytes 983044
  6.5 2.8 %copy-start.3 = (bf16[1,1,128,1280]{3,2,1,0:T(8,128)(2,1)S(1)}, bf16[1,1,128,1280]{3,2,1,0:T(8,128)(2,1)}, u32[]{:S(2)}) copy-start(bf16[1,1,128,1280]{3,2,1,0:T(8,128)(2,1)} %param.12) | copy-start | bytes 983044
  6.5 38.6 %all-gather.5.cloned.1.call-start = ((), (), s32[]{:S(2)}) async-start(), calls=%async_computation.5 | async-start | bytes 1638400 | tf_op jit(solution)/shard_map/all_gather | solution.py:76
  8.5 69.0 %all-gather.7.cloned.1.call-start = ((), (), s32[]{:S(2)}) async-start(), calls=%async_computation.6 | async-start | bytes 1638400 | tf_op jit(solution)/shard_map/all_gather | solution.py:77
  9.2 126.6 %reduce-scatter.2.cloned.1.call-start = ((), (), s32[]{:S(2)}) async-start(), calls=%async_computation.4 | async-start | bytes 3932160 | tf_op jit(solution)/shard_map/reduce_scatter | solution.py:98
  98.9 0.7 copy-start.5
  98.9 0.7 copy-start.6
  98.9 0.8 copy-start.7
  98.9 37.0 %copy-start.2 = (bf16[1,1,128,2560]{3,2,1,0:T(8,128)(2,1)S(1)}, bf16[1,1,128,2560]{3,2,1,0:T(8,128)(2,1)}, u32[]{:S(2)}) copy-start(bf16[1,1,128,2560]{3,2,1,0:T(8,128)(2,1)} %param.15) | copy-start | bytes 1966084
  135.9 6.7 %copy-start.1 = (f32[128,2560]{1,0:T(8,128)S(1)}, f32[128,2560]{1,0:T(8,128)}, u32[]{:S(2)}) copy-start(f32[128,2560]{1,0:T(8,128)} %reduce-scatter.2.cloned.1.call-done) | copy-start | bytes 3932164
  142.6 8.9 %copy-start.8 = (s32[1,4]{1,0:T(1,128)S(1)}, s32[1,4]{1,0:T(1,128)}, u32[]{:S(2)}) copy-start(s32[1,4]{1,0:T(1,128)} %param.23) | copy-start | bytes 52
  142.6 25.8 %copy-start.4 = (f32[1,1,128,32]{2,3,1,0:T(8,128)S(1)}, f32[1,1,128,32]{2,3,1,0:T(8,128)}, u32[]{:S(2)}) copy-start(f32[1,1,128,32]{2,3,1,0:T(8,128)} %param.21) | copy-start | bytes 49156
  152.6 10.7 %all-to-all-start.1 = ((f32[4,1,2048]{2,1,0:T(1,128)}), f32[4,1,2048]{2,1,0:T(1,128)S(1)}, u32[]{:S(2)}, u32[]{:S(2)}) async-start(f32[4,1,2048]{2,1,0:T(1,128)} %reshape.233), calls=%async_computation.2 | async-start | bytes 65536 | tf_op jit(solution)/shard_map/all_to_all | solution.py:128
Sparse Core Ops, SparseCore 0:
  8.9 36.1 all-gather.4
  46.7 30.7 all-gather.6
  99.0 36.7 reduce-scatter.1
